TPU v7x, 128 devices: a whole 4x4x4 slice. The times are simulated.
128 devices in a mesh: ctx: 8 (over y, x_hi), head: 16 (over x_lo, z, core).
Axes of the slice: x: 4 (x_hi: 2, x_lo: 2; x = x_hi * 2 + x_lo), y: 4, z: 4, core: 2. Of those that a mesh axis runs over, the one named last changes fastest.
Arguments:
- queries: bfloat16 [2, 4096, 4096], P(None, 'ctx', 'head'), may hold values from -6 to 6
- keys: bfloat16 [2, 4096, 4096], P(None, 'ctx', 'head'), may hold values from -6 to 6
- values: bfloat16 [2, 4096, 4096], P(None, 'ctx', 'head'), may hold values from -6 to 6
- rates: float32 [16, 2, 4096], P('head', None, 'ctx'), may hold values from 0.05 to 1
- w_gate: float32 [16, 256, 512], P('head'), may hold values from -0.375 to 0.375
- w_up: float32 [16, 256, 512], P('head'), may hold values from -0.375 to 0.375
- w_down: float32 [16, 512, 256], P('head'), may hold values from -0.25 to 0.25
- gains: float32 [16, 256], P('head'), may hold values from 0.25 to 0.6
- out_proj: bfloat16 [4096, 4096], P('head'), may hold values from -0.125 to 0.125
Outputs:
- output: bfloat16 [2, 4096, 4096], P(None, 'ctx', 'head')
All inputs are finite; a program needn't handle non-finite values.
Results may differ from a plain program's by a relative error of at most 0.0051.
Values may be sent and summed in bfloat16 or wider, within the bound.
A program may use at most 128 MiB of HBM per device.

v0:
```python
import jax
import jax.numpy as jnp
from jax import lax
from jax.sharding import PartitionSpec as P

WINDOW = 256
NS_ITERS = 5
highest = lax.Precision.HIGHEST
attn_temp = 5.0
step_size = 0.5
quintic_one = 3.4445
quintic_two = -4.775
quintic_three = 2.0315


def passed_along(value, axis, steps):
    count = lax.axis_size(axis)
    pairs = [(source, (source + steps) % count) for source in range(count)]
    return lax.ppermute(value, axis, pairs)


def unit_rows(matrix):
    return matrix / jnp.sqrt(jnp.sum(matrix * matrix, axis=-1, keepdims=True) + 1e-06)


def exact_dot(left, right):
    return jnp.dot(left, right, precision=highest, preferred_element_type=jnp.float32)


def fast_grads(key_unit, value_rows, rate_rows, w_gate, w_up, w_down):
    gate_pre = exact_dot(key_unit, w_gate)
    up_pre = exact_dot(key_unit, w_up)
    sigma = jax.nn.sigmoid(gate_pre)
    gate_act = gate_pre * sigma
    hidden = gate_act * up_pre
    target = rate_rows[:, None] * value_rows
    grad_down = exact_dot(hidden.T, target)
    back_hidden = exact_dot(target, w_down.T)
    slope = sigma * (1.0 + gate_pre * (1.0 - sigma))
    grad_gate = exact_dot(key_unit.T, back_hidden * up_pre * slope)
    grad_up = exact_dot(key_unit.T, back_hidden * gate_act)
    return jnp.stack([grad_gate, grad_up, grad_down.T])


def quintic_step(gram, iterate):
    poly = quintic_two * gram + quintic_three * jnp.einsum(
        "mij,mjk->mik", gram, gram, precision=highest
    )
    return quintic_one * iterate + jnp.einsum("mij,mjk->mik", poly, iterate, precision=highest)


def orthogonal(grads):
    norms = jnp.sqrt(jnp.sum(grads * grads, axis=(1, 2), keepdims=True)) + 1e-06
    iterate = grads / norms
    for sweep_at in range(NS_ITERS):
        gram = jnp.einsum("mik,mjk->mij", iterate, iterate, precision=highest)
        iterate = quintic_step(gram, iterate)
    return iterate


def apply_fast(query_unit, w_gate, w_up, w_down):
    gate_pre = exact_dot(query_unit, w_gate)
    gate_act = gate_pre * jax.nn.sigmoid(gate_pre)
    return exact_dot(gate_act * exact_dot(query_unit, w_up), w_down)


def band_attention(query_half, ext_keys, ext_values, masked_head):
    local_rows = query_half.shape[0]
    block_rows = min(512, local_rows)
    scores = lax.dot_general(
        query_half, ext_keys, (((1,), (1,)), ((), ())), preferred_element_type=jnp.float32
    )
    query_pos = jnp.arange(block_rows, dtype=jnp.int32)[:, None]
    key_pos = jnp.arange(block_rows + WINDOW, dtype=jnp.int32)[None, :]
    distance = query_pos + WINDOW - key_pos
    valid = (distance >= 0) & (distance < WINDOW)
    if masked_head is not None:
        valid = valid & ((key_pos + 0 >= WINDOW) | jnp.logical_not(masked_head))
    weights = jnp.where(valid, jnp.exp(attn_temp * (scores - 1.0)), 0.0)
    probs = (weights / jnp.sum(weights, axis=-1, keepdims=True)).astype(jnp.bfloat16)
    outputs = jnp.dot(probs, ext_values, preferred_element_type=jnp.float32)
    return outputs


def body(queries, keys, values, rates, w_gate, w_up, w_down, gains, out_proj):
    group_count, local_rows, head_width = queries.shape
    first_device = lax.axis_index("ctx") == 0
    query_unit = unit_rows(queries.astype(jnp.float32))
    key_unit = unit_rows(keys.astype(jnp.float32))
    query_half = query_unit.astype(jnp.bfloat16)
    key_half = key_unit.astype(jnp.bfloat16)
    tails = jnp.stack([key_half[:, local_rows - WINDOW :], values[:, local_rows - WINDOW :]])
    prior = passed_along(tails, "ctx", 1)
    gate_now = w_gate[0]
    up_now = w_up[0]
    down_now = w_down[0]
    mixed = []
    for group_at in range(group_count):
        if group_at == 0:
            halo_rows = prior[:, 0]
            masked_head = first_device
        else:
            halo_rows = jnp.where(first_device, prior[:, group_at - 1], prior[:, group_at])
            masked_head = None
        ext_keys = jnp.concatenate([halo_rows[0], key_half[group_at]], axis=0)
        ext_values = jnp.concatenate([halo_rows[1], values[group_at]], axis=0)
        attended = band_attention(query_half[group_at], ext_keys, ext_values, masked_head)
        grads = fast_grads(
            key_unit[group_at],
            values[group_at].astype(jnp.float32),
            rates[0, group_at],
            gate_now,
            up_now,
            down_now,
        )
        ortho = orthogonal(lax.psum(grads, "ctx"))
        gate_now = gate_now + step_size * ortho[0]
        up_now = up_now + step_size * ortho[1]
        down_now = down_now + step_size * ortho[2].T
        fast_out = apply_fast(query_unit[group_at], gate_now, up_now, down_now)
        normed = (
            fast_out
            * lax.rsqrt(jnp.mean(fast_out * fast_out, axis=-1, keepdims=True) + 1e-05)
            * gains[0]
        )
        mixed.append((attended + normed).astype(jnp.bfloat16))
    combined = jnp.stack(mixed)
    proj_columns = lax.all_to_all(out_proj, "head", split_axis=1, concat_axis=0, tiled=True)
    summed = jnp.einsum(
        "ctf,fo->cto",
        lax.all_gather(combined, "head", axis=2, tiled=True),
        proj_columns,
        preferred_element_type=jnp.float32,
    )
    return summed.astype(jnp.bfloat16)


def solution(mesh):
    return jax.shard_map(
        body,
        mesh=mesh,
        in_specs=(
            P(None, "ctx", "head"),
            P(None, "ctx", "head"),
            P(None, "ctx", "head"),
            P("head", None, "ctx"),
            P("head", None, None),
            P("head", None, None),
            P("head", None, None),
            P("head", None),
            P("head", None),
        ),
        out_specs=P(None, "ctx", "head"),
        check_vma=False,
    )
```

profile of v0, /device:TPU:1, one launch (start us, length us, event | category | flops | bytes accessed | tf_op | source)
XLA Modules:
  0.0 370.9 jit_solution(8970687296122975035)
XLA Ops:
  10.1 3.6 collective-permute-start
  31.4 2.0 fusion.127
  33.4 82.0 %all-reduce.3.cloned.1.call-done = f32[3,256,512]{2,1,0:T(8,128)} async-done(((f32[3,256,512]{2,1,0:T(8,128)}), f32[3,256,512]{2,1,0:T(8,128)}) %all-reduce.3.cloned.1.call-update) | async-done | bytes 1572880 | tf_op jit(solution)/shard_map/psum | solution.py:116
  115.4 1.8 multiply_reduce_fusion.1
  117.3 1.8 fusion.85
  120.1 1.8 multiply_add_fusion.9
  121.9 1.7 fusion.128
  126.1 1.8 fusion.129
  130.4 1.7 fusion.130
  149.0 2.0 fusion.126
  153.2 1.9 multiply_reduce_fusion.3
  155.1 2.0 copy.11
  157.1 2.8 fusion.16
  159.9 83.1 %all-reduce.5.cloned.1.call-done = f32[3,256,512]{2,1,0:T(8,128)} async-done(((f32[3,256,512]{2,1,0:T(8,128)}), f32[3,256,512]{2,1,0:T(8,128)}) %all-reduce.5.cloned.1.call-update) | async-done | bytes 1572880 | tf_op jit(solution)/shard_map/psum | solution.py:116
  243.0 1.8 multiply_reduce_fusion
  244.9 1.8 fusion.86
  247.6 1.8 multiply_add_fusion.4
  252.1 1.8 multiply_add_fusion.3
  253.8 1.7 fusion.133
  264.8 1.8 multiply_add_fusion
  270.3 2.0 fusion.15
  273.4 43.4 %all_to_all.19 = bf16[256,16,256]{2,0,1:T(8,128)(2,1)S(1)} all-to-all(bf16[256,16,256]{2,0,1:T(8,128)(2,1)S(1)} %bitcast.208), channel_id=1, replica_groups=mesh['ctx'=8,'head'=16] {'head'}, dimensions={1} | all-to-all | bytes 4194304 | tf_op jit(solution)/shard_map/all_to_all | solution.py:128
  316.9 40.8 %all-gather.2.cloned.1.call-done = bf16[2,512,4096]{2,1,0:T(8,128)(2,1)} async-done(((bf16[2,512,256]{2,1,0:T(8,128)(2,1)}), bf16[2,512,4096]{2,1,0:T(8,128)(2,1)}) %all-gather.2.cloned.1.call-update) | async-done | bytes 8388624 | tf_op jit(solution)/shard_map/all_gather | solution.py:131
  357.6 6.5 %convolution_convert_fusion = bf16[2,512,256]{2,1,0:T(8,128)(2,1)} fusion(bf16[2,512,4096]{2,1,0:T(8,128)(2,1)} %all-gather.2.cloned.1.call-done, bf16[4096,256,1]{1,0,2:T(8,128)(2,1)S(1)} %bitcast.210), kind=kOutput, calls=%fused_computation.29 | convolution fusion | flops 2147745792 | bytes 11010048 | tf_op jit(solution)/shard_map/ctf,fo->cto/dot_general | solution.py:129
  (116 shorter events, 63.7 us)
Async XLA Ops:
  6.5 2.6 copy-start.5
  6.5 108.9 %all-reduce.3.cloned.1.call-start = ((), (), s32[]{:S(2)}) async-start(), calls=%async_computation.1 | async-start | bytes 3145728 | tf_op jit(solution)/shard_map/psum | solution.py:116
  9.1 4.5 %copy-start.21 = (f32[1,2,512]{2,1,0:T(2,128)S(1)}, f32[1,2,512]{2,1,0:T(2,128)}, u32[]{:S(2)}) copy-start(f32[1,2,512]{2,1,0:T(2,128)} %param.12) | copy-start | bytes 12292
  9.1 4.5 %copy-start = (f32[1,256,512]{2,1,0:T(8,128)S(1)}, f32[1,256,512]{2,1,0:T(8,128)}, u32[]{:S(2)}) copy-start(f32[1,256,512]{2,1,0:T(8,128)} %param.13) | copy-start | bytes 1572868
  9.2 5.5 %copy-start.8 = (f32[1,256,512]{2,1,0:T(8,128)S(1)}, f32[1,256,512]{2,1,0:T(8,128)}, u32[]{:S(2)}) copy-start(f32[1,256,512]{2,1,0:T(8,128)} %param.14) | copy-start | bytes 1572868
  10.1 17.9 %collective-permute-start = (bf16[2,2,256,256]{3,2,1,0:T(8,128)(2,1)}, bf16[2,2,256,256]{3,2,1,0:T(8,128)(2,1)}, u32[]{:S(2)}, u32[]{:S(2)}) collective-permute-start(bf16[2,2,256,256]{3,2,1,0:T(8,128)(2,1)} %pad_maximum_fusion.2), channel_id=1, source_target_pairs={{0,16},{16,32},{32,48},{48,64},{64,80},{80,96},{96,112},{112,0},{1... | collective-permute-start | bytes 1572872 | tf_op jit(solution)/shard_map/ppermute | solution.py:19
  22.1 2.7 copy-start.12
  22.2 220.8 %all-reduce.5.cloned.1.call-start = ((), (), s32[]{:S(2)}) async-start(), calls=%async_computation.2 | async-start | bytes 3145728 | tf_op jit(solution)/shard_map/psum | solution.py:116
  23.4 3.1 copy-start.13
  27.8 5.6 %copy-start.16 = (bf16[2,512,256]{2,1,0:T(8,128)(2,1)}, bf16[2,512,256]{2,1,0:T(8,128)(2,1)S(1)}, u32[]{:S(2)}) copy-start(bf16[2,512,256]{2,1,0:T(8,128)(2,1)S(1)} %get-tuple-element.6) | copy-start | bytes 1572868
  115.4 1.9 copy-start.14
  138.8 1.1 copy-start.9
  139.9 1.5 copy-start.1
  139.9 1.5 copy-start.6
  147.8 1.1 copy-start.18
  147.8 1.1 copy-start.20
  147.9 209.8 %all-gather.2.cloned.1.call-start = ((), (), s32[]{:S(2)}) async-start(), calls=%async_computation.3 | async-start | bytes 8912896 | tf_op jit(solution)/shard_map/all_gather | solution.py:131
  149.0 2.0 copy-start.3
  152.0 1.2 copy-start.2
  153.2 3.9 %copy-start.22 = (f32[1,256]{1,0:T(1,128)S(1)}, f32[1,256]{1,0:T(1,128)}, u32[]{:S(2)}) copy-start(f32[1,256]{1,0:T(1,128)} %param.16) | copy-start | bytes 3076
  243.0 1.9 copy-start.15
  264.8 1.8 copy-start.4
  270.3 2.0 copy-start.19
  270.3 2.9 copy-start.7
  (3 other events, 3.1 us)
Sparse Core Ops, SparseCore 0:
  22.3 93.0 all-reduce.2
  148.0 94.9 all-reduce.4
  273.3 84.2 all-gather.1
where the time goes:
time: 377 us; the launch traced here: 371 us
  waiting for transfers between devices  206 us (55%)
  matrix products  80.6 us (21%)
  blocking collectives  43.4 us (12%)
  other arithmetic  14 us (4%)
  between operations  14 us (4%)
  local copies, waits for them, and re-layouts  8.64 us (2%)
  starting transfers between devices  4.11 us (1%)
    psum x2, waiting for transfers between devices, body(): ortho = orthogonal(lax.psum(grads, 'ctx'))  165 us
    all_to_all x1, blocking collectives, body(): lax.all_to_all(out_proj, 'head', split_axis=1, concat_axis=0, tiled=True)  43.4 us
    all_gather x1, waiting for transfers between devices, body(): lax.all_gather(combined, 'head', axis=2, tiled=True)  40.8 us
    dot_general x18, matrix products, exact_dot(): jnp.dot(left, right, precision=highest, preferred_element_type=jnp.float32)  22.3 us
    dot_general x10, matrix products, orthogonal(): gram = jnp.einsum('mik,mjk->mij', iterate, iterate, precision=highest)  17 us
    dot_general x10, matrix products, quintic_step(): jnp.einsum('mij,mjk->mik', poly, iterate, precision=highest)  16.6 us
    dot_general x10, matrix products, quintic_step(): jnp.einsum('mij,mjk->mik', gram, gram, precision=highest)  9.34 us
  transfers between devices with their start and end apart: 4, of which 4 were waited for; matrix products, arithmetic and copies ran while one was open for 8% of the time, Pallas kernels for 0%

commit v1 on v0

--- a/solution.py
+++ b/solution.py
@@ -128,7 +128,7 @@
     proj_columns = lax.all_to_all(out_proj, "head", split_axis=1, concat_axis=0, tiled=True)
     summed = jnp.einsum(
         "ctf,fo->cto",
-        lax.all_gather(combined, "head", axis=2, tiled=True),
+        jnp.concatenate(lax.all_gather(combined, "head"), axis=2),
         proj_columns,
         preferred_element_type=jnp.float32,
     )

time: 377 us -> 372 us (0.987)
  waiting for transfers between devices: 206 us -> 184 us
  blocking collectives: 43.4 us -> 54.5 us
  local copies, waits for them, and re-layouts: 8.64 us -> 13.8 us
    all_gather x1, waiting for transfers between devices: 40.8 us -> 18.6 us  [body(): lax.all_gather(combined, 'head')]
    all_to_all x1, blocking collectives: 43.4 us -> 54.5 us  [body(): lax.all_to_all(out_proj, 'head', split_axis=1, concat_axis=0, tiled=True)]
  transfers between devices with their start and end apart: 4 -> 4, of which waited for: 4 -> 4; matrix products, arithmetic and copies ran while one was open for 8% -> 10% of each run, Pallas kernels for 0% -> 0%
where the time goes in v1:
time: 372 us; the launch traced here: 366 us
  waiting for transfers between devices  184 us (49%)
  matrix products  81 us (22%)
  blocking collectives  54.5 us (15%)
  between operations  14.2 us (4%)
  other arithmetic  14 us (4%)
  local copies, waits for them, and re-layouts  13.8 us (4%)
  starting transfers between devices  4.11 us (1%)
    psum x2, waiting for transfers between devices, body(): ortho = orthogonal(lax.psum(grads, 'ctx'))  165 us
    all_to_all x1, blocking collectives, body(): lax.all_to_all(out_proj, 'head', split_axis=1, concat_axis=0, tiled=True)  54.5 us
    dot_general x18, matrix products, exact_dot(): jnp.dot(left, right, precision=highest, preferred_element_type=jnp.float32)  22.3 us
    all_gather x1, waiting for transfers between devices, body(): lax.all_gather(combined, 'head')  18.6 us
    dot_general x10, matrix products, orthogonal(): gram = jnp.einsum('mik,mjk->mij', iterate, iterate, precision=highest)  16.9 us
    dot_general x10, matrix products, quintic_step(): jnp.einsum('mij,mjk->mik', poly, iterate, precision=highest)  16.6 us
    dot_general x10, matrix products, quintic_step(): jnp.einsum('mij,mjk->mik', gram, gram, precision=highest)  9.34 us
  transfers between devices with their start and end apart: 4, of which 4 were waited for; matrix products, arithmetic and copies ran while one was open for 10% of the time, Pallas kernels for 0%

profile of v1, /device:TPU:1, one launch (start us, length us, event | category | flops | bytes accessed | tf_op | source)
XLA Modules:
  0.0 365.5 jit_solution(9011398698480807)
XLA Ops:
  10.1 3.6 collective-permute-start
  29.7 1.7 slice_bitcast_fusion.28
  31.4 2.0 fusion.135
  33.4 82.0 %all-reduce.3.cloned.1.call-done = f32[3,256,512]{2,1,0:T(8,128)} async-done(((f32[3,256,512]{2,1,0:T(8,128)}), f32[3,256,512]{2,1,0:T(8,128)}) %all-reduce.3.cloned.1.call-update) | async-done | bytes 1572880 | tf_op jit(solution)/shard_map/psum | solution.py:116
  115.4 1.8 multiply_reduce_fusion.1
  117.3 1.8 fusion.93
  120.0 1.8 multiply_add_fusion.9
  148.9 2.0 fusion.134
  153.2 1.9 multiply_reduce_fusion.3
  155.1 2.0 copy.21
  157.1 2.8 fusion.24
  159.9 83.1 %all-reduce.5.cloned.1.call-done = f32[3,256,512]{2,1,0:T(8,128)} async-done(((f32[3,256,512]{2,1,0:T(8,128)}), f32[3,256,512]{2,1,0:T(8,128)}) %all-reduce.5.cloned.1.call-update) | async-done | bytes 1572880 | tf_op jit(solution)/shard_map/psum | solution.py:116
  242.9 1.8 multiply_reduce_fusion
  244.8 1.8 fusion.94
  247.6 1.8 multiply_add_fusion.4
  252.0 1.8 multiply_add_fusion.3
  253.8 1.7 fusion.141
  264.8 1.8 multiply_add_fusion
  270.3 2.0 fusion.23
  273.2 2.5 copy.23
  275.7 2.8 copy.24
  278.6 54.5 %all_to_all.16 = bf16[256,16,256]{2,0,1:T(8,128)(2,1)} all-to-all(bf16[256,16,256]{2,0,1:T(8,128)(2,1)S(1)} %copy.24), channel_id=1, replica_groups=mesh['ctx'=8,'head'=16] {'head'}, dimensions={1} | all-to-all | bytes 4194304 | tf_op jit(solution)/shard_map/all_to_all | solution.py:128
  333.1 18.6 %all-gather.3.cloned.1.call-done = bf16[32,512,256]{2,1,0:T(8,128)(2,1)} async-done(((bf16[2,512,256]{2,1,0:T(8,128)(2,1)}), bf16[32,512,256]{2,1,0:T(8,128)(2,1)}) %all-gather.3.cloned.1.call-update) | async-done | bytes 8388624 | tf_op jit(solution)/shard_map/all_gather | solution.py:131
  351.7 7.1 %fusion.8 = bf16[2,512,256]{2,1,0:T(8,128)(2,1)} fusion(bf16[2,512,16,256]{3,1,0,2:T(8,128)(2,1)} %bitcast.222, bf16[256,16,256]{2,0,1:T(8,128)(2,1)} %all_to_all.16), kind=kOutput, calls=%fused_computation.31 | convolution fusion | flops 2147745792 | bytes 11010048 | tf_op jit(solution)/shard_map/ctf,fo->cto/dot_general | solution.py:129
  (115 shorter events, 66.8 us)
Async XLA Ops:
  6.5 2.6 copy-start.5
  6.5 108.8 %all-reduce.3.cloned.1.call-start = ((), (), s32[]{:S(2)}) async-start(), calls=%async_computation.1 | async-start | bytes 3145728 | tf_op jit(solution)/shard_map/psum | solution.py:116
  9.1 4.5 %copy-start.20 = (f32[1,2,512]{2,1,0:T(2,128)S(1)}, f32[1,2,512]{2,1,0:T(2,128)}, u32[]{:S(2)}) copy-start(f32[1,2,512]{2,1,0:T(2,128)} %param.12) | copy-start | bytes 12292
  9.1 4.5 %copy-start = (f32[1,256,512]{2,1,0:T(8,128)S(1)}, f32[1,256,512]{2,1,0:T(8,128)}, u32[]{:S(2)}) copy-start(f32[1,256,512]{2,1,0:T(8,128)} %param.13) | copy-start | bytes 1572868
  9.2 5.5 %copy-start.8 = (f32[1,256,512]{2,1,0:T(8,128)S(1)}, f32[1,256,512]{2,1,0:T(8,128)}, u32[]{:S(2)}) copy-start(f32[1,256,512]{2,1,0:T(8,128)} %param.14) | copy-start | bytes 1572868
  10.1 17.9 %collective-permute-start = (bf16[2,2,256,256]{3,2,1,0:T(8,128)(2,1)}, bf16[2,2,256,256]{3,2,1,0:T(8,128)(2,1)}, u32[]{:S(2)}, u32[]{:S(2)}) collective-permute-start(bf16[2,2,256,256]{3,2,1,0:T(8,128)(2,1)} %pad_maximum_fusion.2), channel_id=1, source_target_pairs={{0,16},{16,32},{32,48},{48,64},{64,80},{80,96},{96,112},{112,0},{1... | collective-permute-start | bytes 1572872 | tf_op jit(solution)/shard_map/ppermute | solution.py:19
  22.2 220.8 %all-reduce.5.cloned.1.call-start = ((), (), s32[]{:S(2)}) async-start(), calls=%async_computation.2 | async-start | bytes 3145728 | tf_op jit(solution)/shard_map/psum | solution.py:116
  23.4 3.1 copy-start.12
  27.8 5.6 %copy-start.15 = (bf16[2,512,256]{2,1,0:T(8,128)(2,1)}, bf16[2,512,256]{2,1,0:T(8,128)(2,1)S(1)}, u32[]{:S(2)}) copy-start(bf16[2,512,256]{2,1,0:T(8,128)(2,1)S(1)} %get-tuple-element.6) | copy-start | bytes 1572868
  115.4 1.9 copy-start.13
  138.8 1.1 copy-start.9
  139.9 1.5 copy-start.1
  139.9 1.5 copy-start.6
  147.8 1.1 copy-start.17
  147.8 1.1 copy-start.19
  147.8 203.8 %all-gather.3.cloned.1.call-start = ((), (), s32[]{:S(2)}) async-start(), calls=%async_computation.3 | async-start | bytes 8912896 | tf_op jit(solution)/shard_map/all_gather | solution.py:131
  148.9 2.0 copy-start.3
  150.9 1.1 copy-start.10
  152.0 1.2 copy-start.2
  153.2 4.0 %copy-start.21 = (f32[1,256]{1,0:T(1,128)S(1)}, f32[1,256]{1,0:T(1,128)}, u32[]{:S(2)}) copy-start(f32[1,256]{1,0:T(1,128)} %param.16) | copy-start | bytes 3076
  242.9 1.9 copy-start.14
  264.8 1.8 copy-start.4
  270.3 2.0 copy-start.18
  270.3 2.9 copy-start.7
  (2 other events, 2.1 us)
Sparse Core Ops, SparseCore 0:
  22.3 93.0 all-reduce.2
  148.0 94.9 all-reduce.4
  273.3 78.3 all-gather.2
